TPU v7x, 32 devices: a whole 2x2x4 slice. The times are simulated.
32 devices in a mesh: leaf: 8 (over z, x), vec: 4 (over y, core).
Axes of the slice: x: 2, y: 2, z: 4, core: 2. Of those that a mesh axis runs over, the one named last changes fastest.
Arguments:
- vectors: float32 [32, 65536], P('vec', 'leaf'), may hold values from -15 to 15
- coords: float32 [3, 65536], P(None, 'leaf'), may hold values from 0 to 64, as said below
- leaf_basis: float32 [32, 65536], P(None, 'leaf'), may hold values from -0.375 to 0.375
- node_ops: float32 [496, 32, 128], P('leaf'), may hold values from -0.75 to 0.75
- top_ops: float32 [2, 32, 192], replicated, may hold values from -0.75 to 0.75
- near_target: int32 [1280], P('leaf'), may hold values from 0 to 255, as said below
- near_source: int32 [1280], P('leaf'), may hold values from 0 to 255, as said below
- near_count: int32 [8], P('leaf'), may hold values from 64 to 160, as said below
Outputs:
- product: float32 [32, 65536], P('vec', 'leaf')
- gram_matrix: float32 [32, 32], P(None, 'vec')
Inputs may be any that keep to these rules, and one draw needn't show every extreme that they name: `near_target`: slots of one index of leaf name target leaves of that index only; each aligned block of 32 slots of an index names each of its leaves once; in the first run every leaf is paired with itself, and in the second run the first leaf of each index is paired with the leaf just below it and the last leaf with the leaf just above it, where those exist. `near_source`: A source leaf lies within 4 leaves of its target leaf; no pair repeats within one index of leaf. The first near_count[d] slots of index d are live, the rest are padding; some index fills all 160 slots. `coords`: point k lies in the box of its leaf l = k // 256: first coordinate from 0.25 l to 0.25 (l + 1), the other two from 0 to 1.
All inputs are finite; a program needn't handle non-finite values.
Results may differ from a plain program's by a relative error of at most 0.0003.
Values sent between devices are 32-bit elements; how exact they have to be, the bound alone decides.
A program may use at most 64 MiB of HBM per device.

v0:
```python
import jax
import jax.numpy as jnp
import numpy as np
from jax import lax
from jax.sharding import PartitionSpec as P

PTS = 256
NEAR_REACH = 4
EXACT_ARITHMETIC = lax.Precision.HIGHEST
SIGNAL = 0.1
NUGGET = 0.5
LENGTH = 0.35
EVEN_OFFSETS = (-2, 2, 3)
ODD_OFFSETS = (-3, -2, 2)


def padded_2(block, sides, width):
    for axis, dim in sides:
        count = lax.axis_size(axis)
        forward = [(i, i + 1) for i in range(count - 1)]
        backward = [(target, source) for source, target in forward]
        low = lax.ppermute(
            lax.slice_in_dim(block, block.shape[dim] - width, None, axis=dim), axis, forward
        )
        high = lax.ppermute(lax.slice_in_dim(block, 0, width, axis=dim), axis, backward)
        block = jnp.concatenate([low, block, high], axis=dim)
    return block


def matern(target_pts, source_pts):
    pair_separation = jnp.zeros(
        (target_pts.shape[1], target_pts.shape[2], source_pts.shape[2]), jnp.float32
    )
    for axis_id in range(3):
        spacing = target_pts[axis_id][:, :, None] - source_pts[axis_id][:, None, :]
        pair_separation = pair_separation + spacing * spacing
    scaled = jnp.sqrt(3.0 * pair_separation) / LENGTH
    return SIGNAL * (1.0 + scaled) * jnp.exp(-scaled)


def take_rows(padded, count_nodes, pad_width):
    parity_ids = np.arange(count_nodes) % 2
    gathered = []
    for slot_index in range(3):
        shift_by = np.where(parity_ids == 0, EVEN_OFFSETS[slot_index], ODD_OFFSETS[slot_index])
        gathered.append(padded[np.arange(count_nodes) + shift_by + pad_width])
    return jnp.stack(gathered, axis=1)


def couple_level(padded, operators, count_nodes, pad_width, rank_size):
    sources = take_rows(padded, count_nodes, pad_width)
    blocks = operators[:, :, : 3 * rank_size].reshape(count_nodes, rank_size, 3, rank_size)
    return jnp.einsum("navr,nras->nvs", sources, blocks, precision=EXACT_ARITHMETIC)


def raise_level(incoming_coefficients, operators, rank_size):
    moved = jnp.einsum(
        "nvr,nrs->nvs",
        incoming_coefficients,
        operators[:, :, 3 * rank_size :],
        precision=EXACT_ARITHMETIC,
    )
    return moved[0::2] + moved[1::2]


def lower_level(field_in, operators, rank_size):
    spread = jnp.repeat(field_in, 2, axis=0)
    return jnp.einsum(
        "nvs,nrs->nvr", spread, operators[:, :, 3 * rank_size :], precision=EXACT_ARITHMETIC
    )


def through(incoming_coefficients, operators, position, rank_size):
    return jnp.einsum(
        "...r,rs->...s",
        incoming_coefficients,
        operators[:, position * rank_size : (position + 1) * rank_size],
        precision=EXACT_ARITHMETIC,
    )


def couple_top(partners, operators, parity, rank_size):
    far_left, near_left, near_right, far_right = partners
    outer = jnp.where(
        parity == 0,
        through(far_right, operators, 3, rank_size),
        through(far_left, operators, 0, rank_size),
    )
    return (
        through(near_left, operators, 1, rank_size)
        + through(near_right, operators, 2, rank_size)
        + outer
    )


def raise_pair(left_coef, right_coef, operators, rank_size):
    return through(left_coef, operators, 4, rank_size) + through(
        right_coef, operators, 5, rank_size
    )


def lower_top(field_in, operators, parity, rank_size):
    even_part = jnp.einsum(
        "...s,rs->...r",
        field_in,
        operators[:, 4 * rank_size : 5 * rank_size],
        precision=EXACT_ARITHMETIC,
    )
    odd_part = jnp.einsum(
        "...s,rs->...r",
        field_in,
        operators[:, 5 * rank_size : 6 * rank_size],
        precision=EXACT_ARITHMETIC,
    )
    return jnp.where(parity == 0, even_part, odd_part)


def near_field(window, local_coords, targets, sources, weights, pair_block):
    columns = window.shape[0] - 3
    leaves_dev = local_coords.shape[1]
    step_count = targets.shape[0] // pair_block

    def add_block(accumulated_sum, portion):
        target_ids, source_ids, live_mask = portion
        source_rows = jnp.take(window, source_ids, axis=1)
        target_pts = jnp.take(local_coords, target_ids, axis=1)
        kernel = matern(target_pts, source_rows[columns:])
        contribution = jnp.einsum(
            "vbs,bts->bvt", source_rows[:columns], kernel, precision=EXACT_ARITHMETIC
        )
        selection_mask = (target_ids[:, None] == jnp.arange(leaves_dev)[None, :]).astype(
            jnp.float32
        ) * live_mask[:, None]
        return (
            accumulated_sum
            + jnp.einsum("qs,qhg->hsg", selection_mask, contribution, precision=EXACT_ARITHMETIC),
            None,
        )

    initial = jnp.zeros((columns, leaves_dev, window.shape[2]), jnp.float32)
    portions = (
        targets.reshape(step_count, pair_block),
        sources.reshape(step_count, pair_block),
        weights.reshape(step_count, pair_block),
    )
    accumulated_sum, unused = lax.scan(add_block, initial, portions)
    return accumulated_sum.reshape(columns, leaves_dev * window.shape[2])


def on_device(vectors, coords, leaf_basis, node_ops, top_ops, near_target, near_source, near_count):
    rank_size = leaf_basis.shape[0]
    columns_dev = vectors.shape[0]
    points_dev = vectors.shape[1]
    leaves_dev = points_dev // PTS
    device = lax.axis_index("leaf")
    vec_index = lax.axis_index("vec")
    vec_count = lax.axis_size("vec")
    leaf_count = lax.axis_size("leaf")
    all_columns = lax.all_gather(vectors, "vec", axis=0, tiled=True)
    base_leaf = device * leaves_dev
    slot_ids = jnp.arange(near_target.shape[0], dtype=jnp.int32)
    live_all = (slot_ids < near_count[0]).astype(jnp.float32)
    target_all = near_target - base_leaf
    source_all = near_source - base_leaf + NEAR_REACH
    local_coords = coords.reshape(3, leaves_dev, PTS)
    stacked = jnp.concatenate([all_columns, coords], axis=0)
    window = padded_2(stacked, (("leaf", 1),), NEAR_REACH * PTS)
    window = window.reshape(all_columns.shape[0] + 3, leaves_dev + 2 * NEAR_REACH, PTS)
    share_count = near_target.shape[0] // vec_count
    slot_grid = slot_ids.reshape(share_count, vec_count)
    picked = lax.dynamic_slice_in_dim(slot_grid, vec_index, 1, 1)[:, 0]
    partial_sum = near_field(
        window,
        local_coords,
        target_all[picked],
        source_all[picked],
        live_all[picked],
        share_count // (leaves_dev // vec_count),
    )
    near_part = lax.psum_scatter(partial_sum, "vec", scatter_dimension=0, tiled=True)
    leaf_basis_matrix = leaf_basis.reshape(rank_size, leaves_dev, PTS)
    current = jnp.einsum(
        "vlp,rlp->lvr",
        vectors.reshape(columns_dev, leaves_dev, PTS),
        leaf_basis_matrix,
        precision=EXACT_ARITHMETIC,
    )
    level_ops = []
    level_fields = []
    offset_node = 0
    nodes_here = leaves_dev
    while nodes_here >= 2:
        ops_here = node_ops[offset_node : offset_node + nodes_here]
        rim_width = min(3, nodes_here)
        padded = padded_2(current, (("leaf", 0),), rim_width)
        level_fields.append(couple_level(padded, ops_here, nodes_here, rim_width, rank_size))
        level_ops.append(ops_here)
        current = raise_level(current, ops_here, rank_size)
        offset_node += nodes_here
        nodes_here //= 2
    top_levels = top_ops.shape[0]
    top_fields = []
    all_roots = lax.all_gather(current, "leaf", axis=0, tiled=True)
    for height in range(top_levels):
        padded_top = jnp.pad(all_roots, ((3, 3), (0, 0), (0, 0)))
        node_id = device // (1 << height)
        near_rows = lax.dynamic_slice_in_dim(padded_top, node_id, 7, 0)
        partners = (near_rows[0], near_rows[1], near_rows[5], near_rows[6])
        top_fields.append(couple_top(partners, top_ops[height], node_id % 2, rank_size))
        if height + 1 < top_levels:
            all_roots = raise_pair(all_roots[0::2], all_roots[1::2], top_ops[height], rank_size)
    downward = top_fields[top_levels - 1]
    for height in range(top_levels - 2, -1, -1):
        parity = device // (1 << height) % 2
        downward = top_fields[height] + lower_top(downward, top_ops[height], parity, rank_size)
    downward = downward[None]
    for index_level in range(len(level_fields) - 1, -1, -1):
        downward = level_fields[index_level] + lower_level(
            downward, level_ops[index_level], rank_size
        )
    far_part = jnp.einsum(
        "lvr,rlp->vlp", downward, leaf_basis_matrix, precision=EXACT_ARITHMETIC
    ).reshape(columns_dev, points_dev)
    product = near_part + far_part + NUGGET * vectors
    gram_part = jnp.einsum("ip,jp->ij", all_columns, product, precision=EXACT_ARITHMETIC)
    gram_matrix = lax.psum(gram_part, "leaf") / (leaf_count * points_dev)
    return (product, gram_matrix)


def solution(mesh):
    return jax.shard_map(
        on_device,
        mesh=mesh,
        in_specs=(
            P("vec", "leaf"),
            P(None, "leaf"),
            P(None, "leaf"),
            P("leaf", None, None),
            P(),
            P("leaf"),
            P("leaf"),
            P("leaf"),
        ),
        out_specs=(P("vec", "leaf"), P(None, "vec")),
        check_vma=False,
    )
```

profile of v0, /device:TPU:0, one launch (start us, length us, event | category | flops | bytes accessed | tf_op | source)
XLA Modules:
  0.0 216.0 jit_solution(17568019953974837203)
XLA Ops:
  7.2 2.3 %fusion.55 = f32[32,8,32]{2,1,0:T(8,128)S(1)} fusion(f32[8,32,256]{2,0,1:T(8,128)} %bitcast.178, f32[4,32,8,256]{3,2,1,0:T(8,128)} %bitcast.175), kind=kOutput, calls=%fused_computation.110 | convolution fusion | flops 25165824 | bytes 1343488 | tf_op jit(solution)/shard_map/vlp,rlp->lvr/dot_general | solution.py:182
  11.4 4.9 %collective-permute-start.10 = (f32[2,8,32]{2,1,0:T(8,128)S(1)}, f32[2,8,32]{2,1,0:T(8,128)S(1)}, u32[]{:S(2)}, u32[]{:S(2)}) collective-permute-start(f32[2,8,32]{2,1,0:T(8,128)S(1)} %slice_add_fusion.3), channel_id=1, source_target_pairs={{0,4},{4,8},{8,12},{12,16},{16,20},{20,24},{24,28},{1,5},{5,9},{9,... | collective-permute-start | bytes 6152 | tf_op jit(solution)/shard_map/ppermute | solution.py:22
  16.3 1.3 collective-permute-start.11
  18.3 5.1 %collective-permute-start.8 = (f32[3,8,32]{2,1,0:T(8,128)}, f32[3,8,32]{2,1,0:T(8,128)}, u32[]{:S(2)}, u32[]{:S(2)}) collective-permute-start(f32[3,8,32]{2,1,0:T(8,128)} %get-tuple-element.113), channel_id=1, source_target_pairs={{0,4},{4,8},{8,12},{12,16},{16,20},{20,24},{24,28},{1,5},{5,9},{9,... | collective-permute-start | bytes 9224 | tf_op jit(solution)/shard_map/ppermute | solution.py:22
  24.0 4.4 %collective-permute-start.6 = (f32[3,8,32]{2,1,0:T(8,128)}, f32[3,8,32]{2,1,0:T(8,128)}, u32[]{:S(2)}, u32[]{:S(2)}) collective-permute-start(f32[3,8,32]{2,1,0:T(8,128)} %get-tuple-element.111), channel_id=1, source_target_pairs={{0,4},{4,8},{8,12},{12,16},{16,20},{20,24},{24,28},{1,5},{5,9},{9,... | collective-permute-start | bytes 9224 | tf_op jit(solution)/shard_map/ppermute | solution.py:22
  29.9 31.5 %all_gather.7 = f32[8,8,32]{2,1,0:T(8,128)S(1)} all-gather(f32[1,8,32]{2,1,0:T(8,128)S(1)} %slice_add_fusion.4), channel_id=1, replica_groups=mesh['leaf'=8,'vec'=4] {'leaf'}, dimensions={0}, use_global_device_ids=true | all-gather | bytes 9216 | tf_op jit(solution)/shard_map/all_gather | solution.py:203
  72.6 1.4 reshape.158
  74.0 1.7 reshape.157
  78.4 1.6 collective-permute-start.4
  83.5 1.3 constant_dynamic-update-slice_fusion.1
  84.9 4.6 %collective-permute-start = (f32[35,1024]{1,0:T(8,128)S(1)}, f32[35,1024]{1,0:T(8,128)S(1)}, u32[]{:S(2)}, u32[]{:S(2)}) collective-permute-start(f32[35,1024]{1,0:T(8,128)S(1)} %get-tuple-element.103), channel_id=1, source_target_pairs={{0,4},{4,8},{8,12},{12,16},{16,20},{20,24},{24,28},{1,5},{5,9},{9,... | collective-permute-start | bytes 430088 | tf_op jit(solution)/shard_map/ppermute | solution.py:22
  92.9 5.2 %collective-permute-start.2 = (f32[3,8,32]{2,1,0:T(8,128)}, f32[3,8,32]{2,1,0:T(8,128)S(1)}, u32[]{:S(2)}, u32[]{:S(2)}) collective-permute-start(f32[3,8,32]{2,1,0:T(8,128)} %get-tuple-element.105), channel_id=1, source_target_pairs={{0,4},{4,8},{8,12},{12,16},{16,20},{20,24},{24,28},{1,5},{5,9},{9,... | collective-permute-start | bytes 9224 | tf_op jit(solution)/shard_map/ppermute | solution.py:22
  100.1 1.7 copy.66
  101.8 53.4 %while.11 = (s32[]{:T(128)}, f32[32,32,256]{2,1,0:T(8,128)S(1)}, s32[8,5]{1,0:T(8,128)S(1)}, f32[35,40,256]{2,0,1:T(8,128)}, s32[8,5]{1,0:T(8,128)S(1)}, /*index...) while((s32[]{:T(128)}, f32[32,32,256]{2,1,0:T(8,128)S(1)}, ...), condition=%wide.region_1.2_spmd.clone, body=%wide.region_0.1_spmd.clone.sunk | while | flops 146720672 | bytes 3547571 | solution.py:146
  101.8 2.0 gather_fusion
  104.7 2.4 %fusion.205 = f32[5,32,256]{2,1,0:T(8,128)S(1)} fusion(f32[5,256]{1,0:T(8,128)S(1)} %bitcast.189, f32[5,256]{1,0:T(8,128)S(1)} %bitcast.192, f32[5,256]{1,0:T(8,128)S(1)} %bitcast.190, f32[5,256]{1,0:T(8,128)S(1)} %bitcast.193, f32[5,256]{1,0:T(8,128)S(1)} %bitcast.191, f32[5,256]{1,0:T(8,128)S(1)} %bitcast.194, ...), kind=kOutput, calls=%fused_computation.22.clone.1 | convolution fusion | flops 130416640 | bytes 376832 | tf_op jit(solution)/shard_map/while/body/eval_jaxpr/vbs,bts->bvt/dot_general | solution.py:128
  107.1 1.3 fusion.207
  108.5 2.0 gather_fusion
  111.4 2.4 %fusion.205 = f32[5,32,256]{2,1,0:T(8,128)S(1)} fusion(f32[5,256]{1,0:T(8,128)S(1)} %bitcast.189, f32[5,256]{1,0:T(8,128)S(1)} %bitcast.192, f32[5,256]{1,0:T(8,128)S(1)} %bitcast.190, f32[5,256]{1,0:T(8,128)S(1)} %bitcast.193, f32[5,256]{1,0:T(8,128)S(1)} %bitcast.191, f32[5,256]{1,0:T(8,128)S(1)} %bitcast.194, ...), kind=kOutput, calls=%fused_computation.22.clone.1 | convolution fusion | flops 130416640 | bytes 376832 | tf_op jit(solution)/shard_map/while/body/eval_jaxpr/vbs,bts->bvt/dot_general | solution.py:128
  113.8 1.3 fusion.207
  115.2 2.0 gather_fusion
  118.0 2.4 %fusion.205 = f32[5,32,256]{2,1,0:T(8,128)S(1)} fusion(f32[5,256]{1,0:T(8,128)S(1)} %bitcast.189, f32[5,256]{1,0:T(8,128)S(1)} %bitcast.192, f32[5,256]{1,0:T(8,128)S(1)} %bitcast.190, f32[5,256]{1,0:T(8,128)S(1)} %bitcast.193, f32[5,256]{1,0:T(8,128)S(1)} %bitcast.191, f32[5,256]{1,0:T(8,128)S(1)} %bitcast.194, ...), kind=kOutput, calls=%fused_computation.22.clone.1 | convolution fusion | flops 130416640 | bytes 376832 | tf_op jit(solution)/shard_map/while/body/eval_jaxpr/vbs,bts->bvt/dot_general | solution.py:128
  120.5 1.3 fusion.207
  121.8 2.0 gather_fusion
  124.7 2.4 %fusion.205 = f32[5,32,256]{2,1,0:T(8,128)S(1)} fusion(f32[5,256]{1,0:T(8,128)S(1)} %bitcast.189, f32[5,256]{1,0:T(8,128)S(1)} %bitcast.192, f32[5,256]{1,0:T(8,128)S(1)} %bitcast.190, f32[5,256]{1,0:T(8,128)S(1)} %bitcast.193, f32[5,256]{1,0:T(8,128)S(1)} %bitcast.191, f32[5,256]{1,0:T(8,128)S(1)} %bitcast.194, ...), kind=kOutput, calls=%fused_computation.22.clone.1 | convolution fusion | flops 130416640 | bytes 376832 | tf_op jit(solution)/shard_map/while/body/eval_jaxpr/vbs,bts->bvt/dot_general | solution.py:128
  127.1 1.3 fusion.207
  128.5 2.0 gather_fusion
  131.4 2.4 %fusion.205 = f32[5,32,256]{2,1,0:T(8,128)S(1)} fusion(f32[5,256]{1,0:T(8,128)S(1)} %bitcast.189, f32[5,256]{1,0:T(8,128)S(1)} %bitcast.192, f32[5,256]{1,0:T(8,128)S(1)} %bitcast.190, f32[5,256]{1,0:T(8,128)S(1)} %bitcast.193, f32[5,256]{1,0:T(8,128)S(1)} %bitcast.191, f32[5,256]{1,0:T(8,128)S(1)} %bitcast.194, ...), kind=kOutput, calls=%fused_computation.22.clone.1 | convolution fusion | flops 130416640 | bytes 376832 | tf_op jit(solution)/shard_map/while/body/eval_jaxpr/vbs,bts->bvt/dot_general | solution.py:128
  133.8 1.3 fusion.207
  135.2 2.0 gather_fusion
  138.1 2.4 %fusion.205 = f32[5,32,256]{2,1,0:T(8,128)S(1)} fusion(f32[5,256]{1,0:T(8,128)S(1)} %bitcast.189, f32[5,256]{1,0:T(8,128)S(1)} %bitcast.192, f32[5,256]{1,0:T(8,128)S(1)} %bitcast.190, f32[5,256]{1,0:T(8,128)S(1)} %bitcast.193, f32[5,256]{1,0:T(8,128)S(1)} %bitcast.191, f32[5,256]{1,0:T(8,128)S(1)} %bitcast.194, ...), kind=kOutput, calls=%fused_computation.22.clone.1 | convolution fusion | flops 130416640 | bytes 376832 | tf_op jit(solution)/shard_map/while/body/eval_jaxpr/vbs,bts->bvt/dot_general | solution.py:128
  140.5 1.3 fusion.207
  141.9 2.0 gather_fusion
  144.7 2.4 %fusion.205 = f32[5,32,256]{2,1,0:T(8,128)S(1)} fusion(f32[5,256]{1,0:T(8,128)S(1)} %bitcast.189, f32[5,256]{1,0:T(8,128)S(1)} %bitcast.192, f32[5,256]{1,0:T(8,128)S(1)} %bitcast.190, f32[5,256]{1,0:T(8,128)S(1)} %bitcast.193, f32[5,256]{1,0:T(8,128)S(1)} %bitcast.191, f32[5,256]{1,0:T(8,128)S(1)} %bitcast.194, ...), kind=kOutput, calls=%fused_computation.22.clone.1 | convolution fusion | flops 130416640 | bytes 376832 | tf_op jit(solution)/shard_map/while/body/eval_jaxpr/vbs,bts->bvt/dot_general | solution.py:128
  147.2 1.3 fusion.207
  148.6 2.0 gather_fusion
  151.4 2.4 %fusion.205 = f32[5,32,256]{2,1,0:T(8,128)S(1)} fusion(f32[5,256]{1,0:T(8,128)S(1)} %bitcast.189, f32[5,256]{1,0:T(8,128)S(1)} %bitcast.192, f32[5,256]{1,0:T(8,128)S(1)} %bitcast.190, f32[5,256]{1,0:T(8,128)S(1)} %bitcast.193, f32[5,256]{1,0:T(8,128)S(1)} %bitcast.191, f32[5,256]{1,0:T(8,128)S(1)} %bitcast.194, ...), kind=kOutput, calls=%fused_computation.22.clone.1 | convolution fusion | flops 130416640 | bytes 376832 | tf_op jit(solution)/shard_map/while/body/eval_jaxpr/vbs,bts->bvt/dot_general | solution.py:128
  153.9 1.3 fusion.207
  155.2 1.6 copy.82
  164.8 1.3 gather_fusion.10
  166.1 1.3 gather_fusion.9
  167.4 1.3 gather_fusion.8
  170.2 1.4 gather_fusion.5
  171.5 1.4 convolution_bitcast_fusion.3
  172.9 1.8 convolution_bitcast_fusion.2
  174.8 3.2 %fusion.46 = f32[32,8,32]{2,1,0:T(8,128)S(1)} fusion(f32[32,32,3,32]{3,2,1,0:T(4,128)S(1)} %copy-done.1, f32[32,1,8,32]{3,2,0,1:T(8,128)S(1)} %bitcast.181, f32[32,1,8,32]{3,2,0,1:T(8,128)S(1)} %bitcast.180, f32[32,1,8,32]{3,2,0,1:T(8,128)} %bitcast.182), kind=kOutput, calls=%fused_computation.89 | convolution fusion | flops 9486336 | bytes 524288 | tf_op jit(solution)/shard_map/navr,nras->nvs/dot_general | solution.py:53
  182.2 3.1 %reduce-scatter.2.cloned.1.call-done = f32[8,8192]{1,0:T(8,128)} async-done(((f32[32,8192]{1,0:T(8,128)}), f32[8,8192]{1,0:T(8,128)}) %reduce-scatter.2.cloned.1.call-update) | async-done | bytes 262160 | tf_op jit(solution)/shard_map/reduce_scatter | solution.py:180
  187.2 21.4 %psum.7 = f32[32,8]{0,1:T(8,128)S(1)} all-reduce(f32[32,8]{0,1:T(8,128)S(1)} %convolution_bitcast_fusion.5), channel_id=1, replica_groups=mesh['leaf'=8,'vec'=4] {'leaf'}, use_global_device_ids=true, to_apply=%region_3.4 | all-reduce | flops 256 | bytes 2048 | tf_op jit(solution)/shard_map/psum | solution.py:226
  (301 shorter events, 49.1 us)
Async XLA Ops:
  7.2 2.4 %copy-start = (f32[62,32,128]{2,1,0:T(8,128)S(1)}, f32[62,32,128]{2,1,0:T(8,128)}, u32[]{:S(2)}) copy-start(f32[62,32,128]{2,1,0:T(8,128)} %param.43) | copy-start | bytes 3047428
  7.2 76.3 %all-gather.2.cloned.1.call-start = ((), (), s32[]{:S(2)}) async-start(), calls=%async_computation.1 | async-start | bytes 1310720 | tf_op jit(solution)/shard_map/all_gather | solution.py:159
  9.5 51.9 %copy-start.11 = (f32[2,32,192]{2,1,0:T(8,128)S(1)}, f32[2,32,192]{2,1,0:T(8,128)}, u32[]{:S(2)}) copy-start(f32[2,32,192]{2,1,0:T(8,128)} %param.44) | copy-start | bytes 147460
  9.6 53.6 %copy-start.27 = (s32[4]{0:T(128)S(1)}, s32[4]{0:T(128)}, u32[]{:S(2)}) copy-start(s32[4]{0:T(128)} %constant.214) | copy-start | bytes 52
  9.6 54.2 %copy-start.26 = (s32[8]{0:T(128)S(1)}, s32[8]{0:T(128)}, u32[]{:S(2)}) copy-start(s32[8]{0:T(128)} %constant.211) | copy-start | bytes 100
  9.6 54.8 %copy-start.25 = (s32[16]{0:T(128)S(1)}, s32[16]{0:T(128)}, u32[]{:S(2)}) copy-start(s32[16]{0:T(128)} %constant.208) | copy-start | bytes 196
  9.6 55.4 %copy-start.24 = (s32[32]{0:T(128)S(1)}, s32[32]{0:T(128)}, u32[]{:S(2)}) copy-start(s32[32]{0:T(128)} %constant.205) | copy-start | bytes 388
  10.3 56.1 %copy-start.23 = (s32[2]{0:T(128)S(1)}, s32[2]{0:T(128)}, u32[]{:S(2)}) copy-start(s32[2]{0:T(128)} %constant.217) | copy-start | bytes 28
  10.3 56.1 %copy-start.21 = (s32[4]{0:T(128)S(1)}, s32[4]{0:T(128)}, u32[]{:S(2)}) copy-start(s32[4]{0:T(128)} %constant.215) | copy-start | bytes 52
  10.3 56.1 %copy-start.22 = (s32[4]{0:T(128)S(1)}, s32[4]{0:T(128)}, u32[]{:S(2)}) copy-start(s32[4]{0:T(128)} %constant.216) | copy-start | bytes 52
  10.3 56.7 %copy-start.19 = (s32[8]{0:T(128)S(1)}, s32[8]{0:T(128)}, u32[]{:S(2)}) copy-start(s32[8]{0:T(128)} %constant.212) | copy-start | bytes 100
  10.3 56.7 %copy-start.20 = (s32[8]{0:T(128)S(1)}, s32[8]{0:T(128)}, u32[]{:S(2)}) copy-start(s32[8]{0:T(128)} %constant.213) | copy-start | bytes 100
  10.3 57.3 %copy-start.17 = (s32[16]{0:T(128)S(1)}, s32[16]{0:T(128)}, u32[]{:S(2)}) copy-start(s32[16]{0:T(128)} %constant.209) | copy-start | bytes 196
  10.3 57.3 %copy-start.18 = (s32[16]{0:T(128)S(1)}, s32[16]{0:T(128)}, u32[]{:S(2)}) copy-start(s32[16]{0:T(128)} %constant.210) | copy-start | bytes 196
  10.4 57.9 %copy-start.15 = (s32[32]{0:T(128)S(1)}, s32[32]{0:T(128)}, u32[]{:S(2)}) copy-start(s32[32]{0:T(128)} %constant.206) | copy-start | bytes 388
  10.4 57.9 %copy-start.16 = (s32[32]{0:T(128)S(1)}, s32[32]{0:T(128)}, u32[]{:S(2)}) copy-start(s32[32]{0:T(128)} %constant.207) | copy-start | bytes 388
  10.4 58.5 %copy-start.13 = (s32[160]{0:T(256)S(1)}, s32[160]{0:T(256)}, u32[]{:S(2)}) copy-start(s32[160]{0:T(256)} %param.46) | copy-start | bytes 1924
  10.4 58.5 %copy-start.14 = (s32[160]{0:T(256)S(1)}, s32[160]{0:T(256)}, u32[]{:S(2)}) copy-start(s32[160]{0:T(256)} %param.45) | copy-start | bytes 1924
  11.4 67.0 %collective-permute-start.10 = (f32[2,8,32]{2,1,0:T(8,128)S(1)}, f32[2,8,32]{2,1,0:T(8,128)S(1)}, u32[]{:S(2)}, u32[]{:S(2)}) collective-permute-start(f32[2,8,32]{2,1,0:T(8,128)S(1)} %slice_add_fusion.3), channel_id=1, source_target_pairs={{0,4},{4,8},{8,12},{12,16},{16,20},{20,24},{24,28},{1,5},{5,9},{9,... | collective-permute-start | bytes 6152 | tf_op jit(solution)/shard_map/ppermute | solution.py:22
  16.3 63.7 %collective-permute-start.11 = (f32[2,8,32]{2,1,0:T(8,128)S(1)}, f32[2,8,32]{2,1,0:T(8,128)S(1)}, u32[]{:S(2)}, u32[]{:S(2)}) collective-permute-start(f32[2,8,32]{2,1,0:T(8,128)S(1)} %slice_add_fusion.3), channel_id=1, source_target_pairs={{4,0},{8,4},{12,8},{16,12},{20,16},{24,20},{28,24},{5,1},{9,5},{13... | collective-permute-start | bytes 6152 | tf_op jit(solution)/shard_map/ppermute | solution.py:25
  17.6 167.6 %reduce-scatter.2.cloned.1.call-start = ((), (), s32[]{:S(2)}) async-start(), calls=%async_computation.2 | async-start | bytes 1310720 | tf_op jit(solution)/shard_map/reduce_scatter | solution.py:180
  18.3 138.5 %collective-permute-start.8 = (f32[3,8,32]{2,1,0:T(8,128)}, f32[3,8,32]{2,1,0:T(8,128)}, u32[]{:S(2)}, u32[]{:S(2)}) collective-permute-start(f32[3,8,32]{2,1,0:T(8,128)} %get-tuple-element.113), channel_id=1, source_target_pairs={{0,4},{4,8},{8,12},{12,16},{16,20},{20,24},{24,28},{1,5},{5,9},{9,... | collective-permute-start | bytes 9224 | tf_op jit(solution)/shard_map/ppermute | solution.py:22
  24.0 60.9 %collective-permute-start.6 = (f32[3,8,32]{2,1,0:T(8,128)}, f32[3,8,32]{2,1,0:T(8,128)}, u32[]{:S(2)}, u32[]{:S(2)}) collective-permute-start(f32[3,8,32]{2,1,0:T(8,128)} %get-tuple-element.111), channel_id=1, source_target_pairs={{0,4},{4,8},{8,12},{12,16},{16,20},{20,24},{24,28},{1,5},{5,9},{9,... | collective-permute-start | bytes 9224 | tf_op jit(solution)/shard_map/ppermute | solution.py:22
  28.4 61.1 %collective-permute-start.7 = (f32[3,8,32]{2,1,0:T(8,128)}, f32[3,8,32]{2,1,0:T(8,128)}, u32[]{:S(2)}, u32[]{:S(2)}) collective-permute-start(f32[3,8,32]{2,1,0:T(8,128)} %get-tuple-element.112), channel_id=1, source_target_pairs={{4,0},{8,4},{12,8},{16,12},{20,16},{24,20},{28,24},{5,1},{9,5},{13... | collective-permute-start | bytes 9224 | tf_op jit(solution)/shard_map/ppermute | solution.py:25
  78.3 6.5 %copy-start.7 = (f32[3,8192]{1,0:T(4,128)S(1)}, f32[3,8192]{1,0:T(4,128)}, u32[]{:S(2)}) copy-start(f32[3,8192]{1,0:T(4,128)} %param.41) | copy-start | bytes 294916
  78.4 13.2 %collective-permute-start.4 = (f32[3,8,32]{2,1,0:T(8,128)}, f32[3,8,32]{2,1,0:T(8,128)S(1)}, u32[]{:S(2)}, u32[]{:S(2)}) collective-permute-start(f32[3,8,32]{2,1,0:T(8,128)} %get-tuple-element.107), channel_id=1, source_target_pairs={{0,4},{4,8},{8,12},{12,16},{16,20},{20,24},{24,28},{1,5},{5,9},{9,... | collective-permute-start | bytes 9224 | tf_op jit(solution)/shard_map/ppermute | solution.py:22
  80.0 12.9 %collective-permute-start.5 = (f32[3,8,32]{2,1,0:T(8,128)}, f32[3,8,32]{2,1,0:T(8,128)S(1)}, u32[]{:S(2)}, u32[]{:S(2)}) collective-permute-start(f32[3,8,32]{2,1,0:T(8,128)} %get-tuple-element.108), channel_id=1, source_target_pairs={{4,0},{8,4},{12,8},{16,12},{20,16},{24,20},{28,24},{5,1},{9,5},{13... | collective-permute-start | bytes 9224 | tf_op jit(solution)/shard_map/ppermute | solution.py:25
  83.5 8.1 %copy-start.12 = (f32[3,8,32]{2,1,0:T(8,128)S(1)}, f32[3,8,32]{2,1,0:T(8,128)}, u32[]{:S(2)}) copy-start(f32[3,8,32]{2,1,0:T(8,128)} %get-tuple-element.114) | copy-start | bytes 9220
  84.9 13.1 %collective-permute-start = (f32[35,1024]{1,0:T(8,128)S(1)}, f32[35,1024]{1,0:T(8,128)S(1)}, u32[]{:S(2)}, u32[]{:S(2)}) collective-permute-start(f32[35,1024]{1,0:T(8,128)S(1)} %get-tuple-element.103), channel_id=1, source_target_pairs={{0,4},{4,8},{8,12},{12,16},{16,20},{20,24},{24,28},{1,5},{5,9},{9,... | collective-permute-start | bytes 430088 | tf_op jit(solution)/shard_map/ppermute | solution.py:22
  89.5 9.9 %collective-permute-start.1 = (f32[35,1024]{1,0:T(8,128)S(1)}, f32[35,1024]{1,0:T(8,128)S(1)}, u32[]{:S(2)}, u32[]{:S(2)}) collective-permute-start(f32[35,1024]{1,0:T(8,128)S(1)} %get-tuple-element.104), channel_id=1, source_target_pairs={{4,0},{8,4},{12,8},{16,12},{20,16},{24,20},{28,24},{5,1},{9,5},{13... | collective-permute-start | bytes 430088 | tf_op jit(solution)/shard_map/ppermute | solution.py:25
  91.6 65.3 %collective-permute-start.9 = (f32[3,8,32]{2,1,0:T(8,128)S(1)}, f32[3,8,32]{2,1,0:T(8,128)S(1)}, u32[]{:S(2)}, u32[]{:S(2)}) collective-permute-start(f32[3,8,32]{2,1,0:T(8,128)S(1)} %copy-done.12), channel_id=1, source_target_pairs={{4,0},{8,4},{12,8},{16,12},{20,16},{24,20},{28,24},{5,1},{9,5},{13... | collective-permute-start | bytes 9224 | tf_op jit(solution)/shard_map/ppermute | solution.py:25
  92.9 75.9 %collective-permute-start.2 = (f32[3,8,32]{2,1,0:T(8,128)}, f32[3,8,32]{2,1,0:T(8,128)S(1)}, u32[]{:S(2)}, u32[]{:S(2)}) collective-permute-start(f32[3,8,32]{2,1,0:T(8,128)} %get-tuple-element.105), channel_id=1, source_target_pairs={{0,4},{4,8},{8,12},{12,16},{16,20},{20,24},{24,28},{1,5},{5,9},{9,... | collective-permute-start | bytes 9224 | tf_op jit(solution)/shard_map/ppermute | solution.py:22
  98.1 70.6 %collective-permute-start.3 = (f32[3,8,32]{2,1,0:T(8,128)}, f32[3,8,32]{2,1,0:T(8,128)S(1)}, u32[]{:S(2)}, u32[]{:S(2)}) collective-permute-start(f32[3,8,32]{2,1,0:T(8,128)} %get-tuple-element.106), channel_id=1, source_target_pairs={{4,0},{8,4},{12,8},{16,12},{20,16},{24,20},{28,24},{5,1},{9,5},{13... | collective-permute-start | bytes 9224 | tf_op jit(solution)/shard_map/ppermute | solution.py:25
  157.6 17.1 %copy-start.1 = (f32[32,32,3,32]{3,2,1,0:T(4,128)S(1)}, f32[32,32,3,32]{3,2,1,0:T(4,128)}, u32[]{:S(2)}) copy-start(f32[32,32,3,32]{3,2,1,0:T(4,128)} %reshape.157) | copy-start | bytes 1179652
  174.7 4.6 %copy-start.4 = (f32[16,32,3,32]{3,2,1,0:T(4,128)S(1)}, f32[16,32,3,32]{3,2,1,0:T(4,128)}, u32[]{:S(2)}) copy-start(f32[16,32,3,32]{3,2,1,0:T(4,128)} %reshape.158) | copy-start | bytes 589828
  174.7 4.5 %copy-start.8 = (f32[16,8,32]{2,1,0:T(8,128)S(1)}, f32[16,8,32]{2,1,0:T(8,128)}, u32[]{:S(2)}) copy-start(f32[16,8,32]{2,1,0:T(8,128)} %gather_fusion.10) | copy-start | bytes 49156
  174.7 4.5 %copy-start.9 = (f32[16,8,32]{2,1,0:T(8,128)S(1)}, f32[16,8,32]{2,1,0:T(8,128)}, u32[]{:S(2)}) copy-start(f32[16,8,32]{2,1,0:T(8,128)} %gather_fusion.9) | copy-start | bytes 49156
  174.7 4.5 %copy-start.10 = (f32[16,8,32]{2,1,0:T(8,128)S(1)}, f32[16,8,32]{2,1,0:T(8,128)}, u32[]{:S(2)}) copy-start(f32[16,8,32]{2,1,0:T(8,128)} %gather_fusion.8) | copy-start | bytes 49156
  178.7 2.9 %copy-start.3 = (f32[32,8192]{1,0:T(8,128)S(1)}, f32[32,8192]{1,0:T(8,128)}, u32[]{:S(2)}) copy-start(f32[32,8192]{1,0:T(8,128)} %param.42) | copy-start | bytes 3145732
  180.5 4.8 %copy-start.5 = (f32[8,8192]{1,0:T(8,128)S(1)}, f32[8,8192]{1,0:T(8,128)}, u32[]{:S(2)}) copy-start(f32[8,8192]{1,0:T(8,128)} %param.40) | copy-start | bytes 786436
  181.5 4.7 %copy-start.2 = (f32[32,8192]{1,0:T(8,128)S(1)}, f32[32,8192]{1,0:T(8,128)}, u32[]{:S(2)}) copy-start(f32[32,8192]{1,0:T(8,128)} %all-gather.2.cloned.1.call-done) | copy-start | bytes 3145732
  186.3 22.9 %copy-start.6 = (f32[8,8192]{1,0:T(8,128)}, f32[8,8192]{1,0:T(8,128)S(1)}, u32[]{:S(2)}) copy-start(f32[8,8192]{1,0:T(8,128)S(1)} %multiply_add_fusion) | copy-start | bytes 786436
Sparse Core Ops, SparseCore 0:
  17.8 19.0 all-gather.1
  157.0 28.2 reduce-scatter.1
where the time goes:
time: 217 us; the launch traced here: 216 us
  blocking collectives  52.8 us (24%)
  local copies, waits for them, and re-layouts  52.2 us (24%)
  matrix products  48 us (22%)
  starting transfers between devices  33.5 us (15%)
  between operations  15.5 us (7%)
  other arithmetic  9.62 us (4%)
  waiting for transfers between devices  3.15 us (1%)
    all_gather x1, blocking collectives, on_device(): all_roots = lax.all_gather(current, 'leaf', axis=0, tiled=True)  31.5 us
    ppermute x6, starting transfers between devices, padded_2(): lax.ppermute(lax.slice_in_dim(block, block.shape[dim] - width, None, axis...  25.7 us
    psum x1, blocking collectives, on_device(): gram_matrix = lax.psum(gram_part, 'leaf') / (leaf_count * points_dev)  21.4 us
    dot_general x8, matrix products, add_block(): jnp.einsum('vbs,bts->bvt', source_rows[:columns], kernel, precision=EXACT...  19.2 us
    gather x8, local copies, waits for them, and re-layouts, add_block(): source_rows = jnp.take(window, source_ids, axis=1)  15.9 us
    gather x15, local copies, waits for them, and re-layouts, take_rows(): gathered.append(padded[np.arange(count_nodes) + shift_by + pad_width])  15.6 us
    dot_general x8, matrix products, add_block(): jnp.einsum('qs,qhg->hsg', selection_mask, contribution, precision=EXACT_A...  10.5 us
    dot_general x5, matrix products, couple_level(): jnp.einsum('navr,nras->nvs', sources, blocks, precision=EXACT_ARITHMETIC)  7.84 us
  transfers between devices with their start and end apart: 14, of which 1 were waited for; matrix products, arithmetic and copies ran while one was open for 48% of the time, Pallas kernels for 0%

commit v1 on v0

--- a/solution.py
+++ b/solution.py
@@ -200,7 +200,12 @@
         nodes_here //= 2
     top_levels = top_ops.shape[0]
     top_fields = []
-    all_roots = lax.all_gather(current, "leaf", axis=0, tiled=True)
+    ring = [current]
+    for hop in range(7):
+        ring.append(lax.ppermute(ring[-1], "leaf", [(dev, (dev + 1) % 8) for dev in range(8)]))
+    all_roots = jnp.roll(
+        jnp.concatenate(ring[::-1], axis=0), (lax.axis_index("leaf") + 1) * ring[0].shape[0], axis=0
+    )
     for height in range(top_levels):
         padded_top = jnp.pad(all_roots, ((3, 3), (0, 0), (0, 0)))
         node_id = device // (1 << height)

time: 217 us -> 303 us (1.40)
  other arithmetic: 9.62 us -> 45.1 us
  blocking collectives: 52.8 us -> 21.4 us
  local copies, waits for them, and re-layouts: 52.2 us -> 83.3 us
  waiting for transfers between devices: 3.15 us -> 31.2 us
  starting transfers between devices: 33.5 us -> 45.2 us
  matrix products: 48 us -> 56.9 us
    all_gather x1 -> x0, blocking collectives: 31.5 us -> none  [on_device(): all_roots = lax.all_gather(current, 'leaf', axis=0, tiled=True)]
    reduce_scatter x1, waiting for transfers between devices: 3.09 us -> 20.3 us  [on_device(): lax.psum_scatter(partial_sum, 'vec', scatter_dimension=0, tiled=True)]
    ppermute x0 -> x7, starting transfers between devices: none -> 13.2 us  [on_device(): lax.ppermute(ring[-1], 'leaf', [(dev, (dev + 1) % 8) for dev in range(8)])]
    select_n x16, other arithmetic: 0.76 us -> 10.9 us  [add_block(): source_rows = jnp.take(window, source_ids, axis=1)]
    and x8, other arithmetic: 0.13 us -> 9.75 us  [add_block(): target_pts = jnp.take(local_coords, target_ids, axis=1)]
    gather x8, local copies, waits for them, and re-layouts: 4.59 us -> 11.8 us  [add_block(): target_pts = jnp.take(local_coords, target_ids, axis=1)]
    unnamed x60 -> x100, local copies, waits for them, and re-layouts: 5.28 us -> 11.3 us
    ppermute x0 -> x7, waiting for transfers between devices: none -> 5.8 us  [on_device(): lax.ppermute(ring[-1], 'leaf', [(dev, (dev + 1) % 8) for dev in range(8)])]
  transfers between devices with their start and end apart: 14 -> 21, of which waited for: 1 -> 5; matrix products, arithmetic and copies ran while one was open for 48% -> 24% of each run, Pallas kernels for 0% -> 0%
where the time goes in v1:
time: 303 us; the launch traced here: 300 us
  local copies, waits for them, and re-layouts  83.3 us (27%)
  matrix products  56.9 us (19%)
  starting transfers between devices  45.2 us (15%)
  other arithmetic  45.1 us (15%)
  waiting for transfers between devices  31.2 us (10%)
  blocking collectives  21.4 us (7%)
  between operations  15.5 us (5%)
    ppermute x6, starting transfers between devices, padded_2(): lax.ppermute(lax.slice_in_dim(block, block.shape[dim] - width, None, axis...  24.1 us
    psum x1, blocking collectives, on_device(): gram_matrix = lax.psum(gram_part, 'leaf') / (leaf_count * points_dev)  21.4 us
    gather x15, local copies, waits for them, and re-layouts, take_rows(): gathered.append(padded[np.arange(count_nodes) + shift_by + pad_width])  21 us
    reduce_scatter x1, waiting for transfers between devices, on_device(): lax.psum_scatter(partial_sum, 'vec', scatter_dimension=0, tiled=True)  20.3 us
    dot_general x8, matrix products, add_block(): jnp.einsum('vbs,bts->bvt', source_rows[:columns], kernel, precision=EXACT...  19.2 us
    gather x8, local copies, waits for them, and re-layouts, add_block(): source_rows = jnp.take(window, source_ids, axis=1)  15.9 us
    dot_general x8, matrix products, add_block(): jnp.einsum('qs,qhg->hsg', selection_mask, contribution, precision=EXACT_A...  15.4 us
    ppermute x7, starting transfers between devices, on_device(): lax.ppermute(ring[-1], 'leaf', [(dev, (dev + 1) % 8) for dev in range(8)])  13.2 us
  transfers between devices with their start and end apart: 21, of which 5 were waited for; matrix products, arithmetic and copies ran while one was open for 24% of the time, Pallas kernels for 0%

profile of v1, /device:TPU:0, one launch (start us, length us, event | category | flops | bytes accessed | tf_op | source)
XLA Modules:
  0.0 299.6 jit_solution(9275663300006718576)
XLA Ops:
  7.2 2.3 fusion.55
  11.4 5.5 %collective-permute-start.10 = (f32[2,8,32]{2,1,0:T(8,128)S(1)}, f32[2,8,32]{2,1,0:T(8,128)}, u32[]{:S(2)}, u32[]{:S(2)}) collective-permute-start(f32[2,8,32]{2,1,0:T(8,128)S(1)} %slice_add_fusion.3), channel_id=1, source_target_pairs={{0,4},{4,8},{8,12},{12,16},{16,20},{20,24},{24,28},{1,5},{5,9},{9,... | collective-permute-start | bytes 6152 | tf_op jit(solution)/shard_map/ppermute | solution.py:22
  19.1 2.6 collective-permute-start.12
  22.3 4.4 %collective-permute-start.8 = (f32[3,8,32]{2,1,0:T(8,128)}, f32[3,8,32]{2,1,0:T(8,128)}, u32[]{:S(2)}, u32[]{:S(2)}) collective-permute-start(f32[3,8,32]{2,1,0:T(8,128)} %get-tuple-element.106), channel_id=1, source_target_pairs={{0,4},{4,8},{8,12},{12,16},{16,20},{20,24},{24,28},{1,5},{5,9},{9,... | collective-permute-start | bytes 9224 | tf_op jit(solution)/shard_map/ppermute | solution.py:22
  43.6 3.1 %reshape.157 = f32[32,32,3,32]{3,2,1,0:T(4,128)} reshape(f32[32,32,96]{2,1,0:T(8,128)} %slice.211) | data formatting | bytes 786432 | tf_op jit(solution)/shard_map/reshape | solution.py:52
  51.7 5.1 %collective-permute-start.6 = (f32[3,8,32]{2,1,0:T(8,128)}, f32[3,8,32]{2,1,0:T(8,128)}, u32[]{:S(2)}, u32[]{:S(2)}) collective-permute-start(f32[3,8,32]{2,1,0:T(8,128)} %get-tuple-element.104), channel_id=1, source_target_pairs={{0,4},{4,8},{8,12},{12,16},{16,20},{20,24},{24,28},{1,5},{5,9},{9,... | collective-permute-start | bytes 9224 | tf_op jit(solution)/shard_map/ppermute | solution.py:22
  58.1 2.7 collective-permute-start.13
  67.3 3.1 %collective-permute-start.2 = (f32[3,8,32]{2,1,0:T(8,128)}, f32[3,8,32]{2,1,0:T(8,128)S(1)}, u32[]{:S(2)}, u32[]{:S(2)}) collective-permute-start(f32[3,8,32]{2,1,0:T(8,128)} %get-tuple-element.98), channel_id=1, source_target_pairs={{0,4},{4,8},{8,12},{12,16},{16,20},{20,24},{24,28},{1,5},{5,9},{9,... | collective-permute-start | bytes 9224 | tf_op jit(solution)/shard_map/ppermute | solution.py:22
  71.8 2.7 collective-permute-start.14
  79.1 4.0 %collective-permute-start.4 = (f32[3,8,32]{2,1,0:T(8,128)}, f32[3,8,32]{2,1,0:T(8,128)}, u32[]{:S(2)}, u32[]{:S(2)}) collective-permute-start(f32[3,8,32]{2,1,0:T(8,128)} %get-tuple-element.100), channel_id=1, source_target_pairs={{0,4},{4,8},{8,12},{12,16},{16,20},{20,24},{24,28},{1,5},{5,9},{9,... | collective-permute-start | bytes 9224 | tf_op jit(solution)/shard_map/ppermute | solution.py:22
  85.0 2.6 collective-permute-start.15
  92.5 4.7 %fusion.46 = f32[32,8,32]{2,1,0:T(8,128)} fusion(f32[32,32,3,32]{3,2,1,0:T(4,128)} %reshape.157, f32[32,1,8,32]{3,2,0,1:T(8,128)} %bitcast.181, f32[32,1,8,32]{3,2,0,1:T(8,128)} %bitcast.180, f32[32,1,8,32]{3,2,0,1:T(8,128)} %bitcast.182), kind=kOutput, calls=%fused_computation.89 | convolution fusion | flops 9486336 | bytes 524288 | tf_op jit(solution)/shard_map/navr,nras->nvs/dot_general | solution.py:53
  97.2 2.1 convolution_bitcast_fusion.2
  99.3 1.8 collective-permute-start.16
  105.4 2.0 gather_fusion.14
  108.2 1.7 convolution_bitcast_fusion.3
  109.9 4.0 %collective-permute-done.17 = f32[1,8,32]{2,1,0:T(8,128)} collective-permute-done((f32[1,8,32]{2,1,0:T(8,128)S(1)}, f32[1,8,32]{2,1,0:T(8,128)}, u32[]{:S(2)}, u32[]{:S(2)}) %collective-permute-start.17) | collective-permute-done | bytes 1056 | tf_op jit(solution)/shard_map/ppermute | solution.py:205
  118.6 1.8 collective-permute-done.18
  129.6 1.9 collective-permute-start
  134.3 4.4 %collective-permute-done.1 = f32[35,1024]{1,0:T(8,128)S(1)} collective-permute-done((f32[35,1024]{1,0:T(8,128)S(1)}, f32[35,1024]{1,0:T(8,128)S(1)}, u32[]{:S(2)}, u32[]{:S(2)}) %collective-permute-start.1) | collective-permute-done | bytes 143392 | tf_op jit(solution)/shard_map/ppermute | solution.py:25
  139.5 1.6 copy.57
  141.1 100.8 %while.11 = (s32[]{:T(128)}, f32[32,32,256]{2,1,0:T(8,128)S(1)}, s32[8,5]{1,0:T(8,128)}, f32[35,40,256]{2,0,1:T(8,128)}, s32[8,5]{1,0:T(8,128)}, /*index=5*/f32[...) while((s32[]{:T(128)}, f32[32,32,256]{2,1,0:T(8,128)S(1)}, ...), condition=%wide.region_1.2_spmd.clone, body=%wide.region_0.1_spmd.clone.sunk | while | flops 146720672 | bytes 3940823 | solution.py:146
  142.4 2.0 gather_fusion
  148.6 2.4 fusion.205
  151.8 1.9 fusion.207
  155.0 2.0 gather_fusion
  161.2 2.4 fusion.205
  164.4 1.9 fusion.207
  167.6 2.0 gather_fusion
  173.8 2.4 fusion.205
  177.0 1.9 fusion.207
  180.2 2.0 gather_fusion
  186.4 2.4 fusion.205
  189.6 1.9 fusion.207
  192.8 2.0 gather_fusion
  199.0 2.4 fusion.205
  202.2 1.9 fusion.207
  205.4 2.0 gather_fusion
  211.6 2.4 fusion.205
  214.8 1.9 fusion.207
  218.0 2.0 gather_fusion
  224.2 2.4 fusion.205
  227.4 1.9 fusion.207
  230.6 2.0 gather_fusion
  236.8 2.4 fusion.205
  240.0 1.9 fusion.207
  248.5 20.3 %reduce-scatter.2.cloned.1.call-done = f32[8,8192]{1,0:T(8,128)} async-done(((f32[32,8192]{1,0:T(8,128)}), f32[8,8192]{1,0:T(8,128)}) %reduce-scatter.2.cloned.1.call-update) | async-done | bytes 262160 | tf_op jit(solution)/shard_map/reduce_scatter | solution.py:180
  270.7 21.4 %psum.7 = f32[32,8]{0,1:T(8,128)S(1)} all-reduce(f32[32,8]{0,1:T(8,128)S(1)} %convolution_bitcast_fusion.5), channel_id=1, replica_groups=mesh['leaf'=8,'vec'=4] {'leaf'}, use_global_device_ids=true, to_apply=%region_3.4 | all-reduce | flops 256 | bytes 2048 | tf_op jit(solution)/shard_map/psum | solution.py:231
  (373 shorter events, 126.4 us)
Async XLA Ops:
  7.2 121.0 %all-gather.2.cloned.1.call-start = ((), (), s32[]{:S(2)}) async-start(), calls=%async_computation.1 | async-start | bytes 1310720 | tf_op jit(solution)/shard_map/all_gather | solution.py:159
  9.5 20.3 %copy-start.19 = (f32[2,32,192]{2,1,0:T(8,128)S(1)}, f32[2,32,192]{2,1,0:T(8,128)}, u32[]{:S(2)}) copy-start(f32[2,32,192]{2,1,0:T(8,128)} %param.44) | copy-start | bytes 147460
  9.6 21.6 %copy-start.41 = (s32[4]{0:T(128)S(1)}, s32[4]{0:T(128)}, u32[]{:S(2)}) copy-start(s32[4]{0:T(128)} %constant.235) | copy-start | bytes 52
  9.6 22.2 %copy-start.40 = (s32[8]{0:T(128)S(1)}, s32[8]{0:T(128)}, u32[]{:S(2)}) copy-start(s32[8]{0:T(128)} %constant.232) | copy-start | bytes 100
  9.6 22.7 %copy-start.39 = (s32[16]{0:T(128)S(1)}, s32[16]{0:T(128)}, u32[]{:S(2)}) copy-start(s32[16]{0:T(128)} %constant.229) | copy-start | bytes 196
  9.6 23.3 %copy-start.38 = (s32[32]{0:T(128)S(1)}, s32[32]{0:T(128)}, u32[]{:S(2)}) copy-start(s32[32]{0:T(128)} %constant.226) | copy-start | bytes 388
  9.6 25.2 %copy-start.37 = (s32[2]{0:T(128)S(1)}, s32[2]{0:T(128)}, u32[]{:S(2)}) copy-start(s32[2]{0:T(128)} %constant.238) | copy-start | bytes 28
  9.6 25.8 %copy-start.35 = (s32[4]{0:T(128)S(1)}, s32[4]{0:T(128)}, u32[]{:S(2)}) copy-start(s32[4]{0:T(128)} %constant.236) | copy-start | bytes 52
  9.6 25.8 %copy-start.36 = (s32[4]{0:T(128)S(1)}, s32[4]{0:T(128)}, u32[]{:S(2)}) copy-start(s32[4]{0:T(128)} %constant.237) | copy-start | bytes 52
  9.6 26.4 %copy-start.33 = (s32[8]{0:T(128)S(1)}, s32[8]{0:T(128)}, u32[]{:S(2)}) copy-start(s32[8]{0:T(128)} %constant.233) | copy-start | bytes 100
  9.7 26.4 %copy-start.34 = (s32[8]{0:T(128)S(1)}, s32[8]{0:T(128)}, u32[]{:S(2)}) copy-start(s32[8]{0:T(128)} %constant.234) | copy-start | bytes 100
  9.7 26.9 %copy-start.31 = (s32[16]{0:T(128)S(1)}, s32[16]{0:T(128)}, u32[]{:S(2)}) copy-start(s32[16]{0:T(128)} %constant.230) | copy-start | bytes 196
  9.7 26.9 %copy-start.32 = (s32[16]{0:T(128)S(1)}, s32[16]{0:T(128)}, u32[]{:S(2)}) copy-start(s32[16]{0:T(128)} %constant.231) | copy-start | bytes 196
  9.7 27.5 %copy-start.29 = (s32[32]{0:T(128)S(1)}, s32[32]{0:T(128)}, u32[]{:S(2)}) copy-start(s32[32]{0:T(128)} %constant.227) | copy-start | bytes 388
  9.7 27.5 %copy-start.30 = (s32[32]{0:T(128)S(1)}, s32[32]{0:T(128)}, u32[]{:S(2)}) copy-start(s32[32]{0:T(128)} %constant.228) | copy-start | bytes 388
  9.7 28.1 %copy-start.27 = (s32[160]{0:T(256)S(1)}, s32[160]{0:T(256)}, u32[]{:S(2)}) copy-start(s32[160]{0:T(256)} %param.46) | copy-start | bytes 1924
  9.7 28.1 %copy-start.28 = (s32[160]{0:T(256)S(1)}, s32[160]{0:T(256)}, u32[]{:S(2)}) copy-start(s32[160]{0:T(256)} %param.45) | copy-start | bytes 1924
  11.4 45.4 %collective-permute-start.10 = (f32[2,8,32]{2,1,0:T(8,128)S(1)}, f32[2,8,32]{2,1,0:T(8,128)}, u32[]{:S(2)}, u32[]{:S(2)}) collective-permute-start(f32[2,8,32]{2,1,0:T(8,128)S(1)} %slice_add_fusion.3), channel_id=1, source_target_pairs={{0,4},{4,8},{8,12},{12,16},{16,20},{20,24},{24,28},{1,5},{5,9},{9,... | collective-permute-start | bytes 6152 | tf_op jit(solution)/shard_map/ppermute | solution.py:22
  16.9 41.2 %collective-permute-start.11 = (f32[2,8,32]{2,1,0:T(8,128)S(1)}, f32[2,8,32]{2,1,0:T(8,128)}, u32[]{:S(2)}, u32[]{:S(2)}) collective-permute-start(f32[2,8,32]{2,1,0:T(8,128)S(1)} %slice_add_fusion.3), channel_id=1, source_target_pairs={{4,0},{8,4},{12,8},{16,12},{20,16},{24,20},{28,24},{5,1},{9,5},{13... | collective-permute-start | bytes 6152 | tf_op jit(solution)/shard_map/ppermute | solution.py:25
  18.2 250.6 %reduce-scatter.2.cloned.1.call-start = ((), (), s32[]{:S(2)}) async-start(), calls=%async_computation.2 | async-start | bytes 1310720 | tf_op jit(solution)/shard_map/reduce_scatter | solution.py:180
  18.5 20.1 %copy-start.16 = (f32[2,8,32]{2,1,0:T(8,128)}, f32[2,8,32]{2,1,0:T(8,128)S(1)}, u32[]{:S(2)}) copy-start(f32[2,8,32]{2,1,0:T(8,128)S(1)} %fusion.97) | copy-start | bytes 6148
  19.1 32.6 %collective-permute-start.12 = (f32[1,8,32]{2,1,0:T(8,128)}, f32[1,8,32]{2,1,0:T(8,128)S(1)}, u32[]{:S(2)}, u32[]{:S(2)}) collective-permute-start(f32[1,8,32]{2,1,0:T(8,128)} %slice_add_fusion.4), channel_id=1, source_target_pairs={{0,4},{4,8},{8,12},{12,16},{16,20},{20,24},{24,28},{28,0},{1,5},{5... | collective-permute-start | bytes 3080 | tf_op jit(solution)/shard_map/ppermute | solution.py:205
  22.3 78.8 %collective-permute-start.8 = (f32[3,8,32]{2,1,0:T(8,128)}, f32[3,8,32]{2,1,0:T(8,128)}, u32[]{:S(2)}, u32[]{:S(2)}) collective-permute-start(f32[3,8,32]{2,1,0:T(8,128)} %get-tuple-element.106), channel_id=1, source_target_pairs={{0,4},{4,8},{8,12},{12,16},{16,20},{20,24},{24,28},{1,5},{5,9},{9,... | collective-permute-start | bytes 9224 | tf_op jit(solution)/shard_map/ppermute | solution.py:22
  26.7 74.5 %collective-permute-start.9 = (f32[3,8,32]{2,1,0:T(8,128)}, f32[3,8,32]{2,1,0:T(8,128)}, u32[]{:S(2)}, u32[]{:S(2)}) collective-permute-start(f32[3,8,32]{2,1,0:T(8,128)} %get-tuple-element.107), channel_id=1, source_target_pairs={{4,0},{8,4},{12,8},{16,12},{20,16},{24,20},{28,24},{5,1},{9,5},{13... | collective-permute-start | bytes 9224 | tf_op jit(solution)/shard_map/ppermute | solution.py:25
  46.8 19.6 %copy-start.10 = (f32[2,32,3,32]{3,2,1,0:T(4,128)S(1)}, f32[2,32,3,32]{3,2,1,0:T(4,128)}, u32[]{:S(2)}) copy-start(f32[2,32,3,32]{3,2,1,0:T(4,128)} %reshape.161) | copy-start | bytes 73732
  51.7 32.7 %copy-start.22 = (f32[1,8,32]{2,1,0:T(8,128)}, f32[1,8,32]{2,1,0:T(8,128)S(1)}, u32[]{:S(2)}) copy-start(f32[1,8,32]{2,1,0:T(8,128)S(1)} %collective-permute-done.12) | copy-start | bytes 3076
  51.7 18.8 %collective-permute-start.6 = (f32[3,8,32]{2,1,0:T(8,128)}, f32[3,8,32]{2,1,0:T(8,128)}, u32[]{:S(2)}, u32[]{:S(2)}) collective-permute-start(f32[3,8,32]{2,1,0:T(8,128)} %get-tuple-element.104), channel_id=1, source_target_pairs={{0,4},{4,8},{8,12},{12,16},{16,20},{20,24},{24,28},{1,5},{5,9},{9,... | collective-permute-start | bytes 9224 | tf_op jit(solution)/shard_map/ppermute | solution.py:22
  56.8 14.9 %collective-permute-start.7 = (f32[3,8,32]{2,1,0:T(8,128)}, f32[3,8,32]{2,1,0:T(8,128)}, u32[]{:S(2)}, u32[]{:S(2)}) collective-permute-start(f32[3,8,32]{2,1,0:T(8,128)} %get-tuple-element.105), channel_id=1, source_target_pairs={{4,0},{8,4},{12,8},{16,12},{20,16},{24,20},{28,24},{5,1},{9,5},{13... | collective-permute-start | bytes 9224 | tf_op jit(solution)/shard_map/ppermute | solution.py:25
  58.1 9.2 %collective-permute-start.13 = (f32[1,8,32]{2,1,0:T(8,128)S(1)}, f32[1,8,32]{2,1,0:T(8,128)}, u32[]{:S(2)}, u32[]{:S(2)}) collective-permute-start(f32[1,8,32]{2,1,0:T(8,128)S(1)} %collective-permute-done.12), channel_id=1, source_target_pairs={{0,4},{4,8},{8,12},{12,16},{16,20},{20,24},{24,28},{28,0},{1,5},{5... | collective-permute-start | bytes 3080 | tf_op jit(solution)/shard_map/ppermute | solution.py:205
  67.3 15.8 %collective-permute-start.2 = (f32[3,8,32]{2,1,0:T(8,128)}, f32[3,8,32]{2,1,0:T(8,128)S(1)}, u32[]{:S(2)}, u32[]{:S(2)}) collective-permute-start(f32[3,8,32]{2,1,0:T(8,128)} %get-tuple-element.98), channel_id=1, source_target_pairs={{0,4},{4,8},{8,12},{12,16},{16,20},{20,24},{24,28},{1,5},{5,9},{9,... | collective-permute-start | bytes 9224 | tf_op jit(solution)/shard_map/ppermute | solution.py:22
  70.4 13.9 %collective-permute-start.3 = (f32[3,8,32]{2,1,0:T(8,128)}, f32[3,8,32]{2,1,0:T(8,128)S(1)}, u32[]{:S(2)}, u32[]{:S(2)}) collective-permute-start(f32[3,8,32]{2,1,0:T(8,128)} %get-tuple-element.99), channel_id=1, source_target_pairs={{4,0},{8,4},{12,8},{16,12},{20,16},{24,20},{28,24},{5,1},{9,5},{13... | collective-permute-start | bytes 9224 | tf_op jit(solution)/shard_map/ppermute | solution.py:25
  71.8 7.3 %collective-permute-start.14 = (f32[1,8,32]{2,1,0:T(8,128)}, f32[1,8,32]{2,1,0:T(8,128)}, u32[]{:S(2)}, u32[]{:S(2)}) collective-permute-start(f32[1,8,32]{2,1,0:T(8,128)} %collective-permute-done.13), channel_id=1, source_target_pairs={{0,4},{4,8},{8,12},{12,16},{16,20},{20,24},{24,28},{28,0},{1,5},{5... | collective-permute-start | bytes 3080 | tf_op jit(solution)/shard_map/ppermute | solution.py:205
  79.1 34.9 %collective-permute-start.4 = (f32[3,8,32]{2,1,0:T(8,128)}, f32[3,8,32]{2,1,0:T(8,128)}, u32[]{:S(2)}, u32[]{:S(2)}) collective-permute-start(f32[3,8,32]{2,1,0:T(8,128)} %get-tuple-element.100), channel_id=1, source_target_pairs={{0,4},{4,8},{8,12},{12,16},{16,20},{20,24},{24,28},{1,5},{5,9},{9,... | collective-permute-start | bytes 9224 | tf_op jit(solution)/shard_map/ppermute | solution.py:22
  83.1 30.8 %collective-permute-start.5 = (f32[3,8,32]{2,1,0:T(8,128)}, f32[3,8,32]{2,1,0:T(8,128)}, u32[]{:S(2)}, u32[]{:S(2)}) collective-permute-start(f32[3,8,32]{2,1,0:T(8,128)} %get-tuple-element.101), channel_id=1, source_target_pairs={{4,0},{8,4},{12,8},{16,12},{20,16},{24,20},{28,24},{5,1},{9,5},{13... | collective-permute-start | bytes 9224 | tf_op jit(solution)/shard_map/ppermute | solution.py:25
  85.0 14.3 %collective-permute-start.15 = (f32[1,8,32]{2,1,0:T(8,128)}, f32[1,8,32]{2,1,0:T(8,128)}, u32[]{:S(2)}, u32[]{:S(2)}) collective-permute-start(f32[1,8,32]{2,1,0:T(8,128)} %collective-permute-done.14), channel_id=1, source_target_pairs={{0,4},{4,8},{8,12},{12,16},{16,20},{20,24},{24,28},{28,0},{1,5},{5... | collective-permute-start | bytes 3080 | tf_op jit(solution)/shard_map/ppermute | solution.py:205
  92.5 4.7 %copy-start.4 = (f32[8,32,3,32]{3,2,1,0:T(4,128)S(1)}, f32[8,32,3,32]{3,2,1,0:T(4,128)}, u32[]{:S(2)}) copy-start(f32[8,32,3,32]{3,2,1,0:T(4,128)} %reshape.159) | copy-start | bytes 294916
  92.5 15.7 %copy-start.6 = (f32[4,32,3,32]{3,2,1,0:T(4,128)S(1)}, f32[4,32,3,32]{3,2,1,0:T(4,128)}, u32[]{:S(2)}) copy-start(f32[4,32,3,32]{3,2,1,0:T(4,128)} %reshape.160) | copy-start | bytes 147460
  97.2 25.9 %copy-start.23 = (f32[1,8,32]{2,1,0:T(8,128)S(1)}, f32[1,8,32]{2,1,0:T(8,128)}, u32[]{:S(2)}) copy-start(f32[1,8,32]{2,1,0:T(8,128)} %copy-done.22) | copy-start | bytes 3076
  97.2 25.9 %copy-start.17 = (f32[2,8,32]{2,1,0:T(8,128)S(1)}, f32[2,8,32]{2,1,0:T(8,128)}, u32[]{:S(2)}) copy-start(f32[2,8,32]{2,1,0:T(8,128)} %copy-done.16) | copy-start | bytes 6148
  97.2 29.0 %copy-start.11 = (f32[32,192]{1,0:T(8,128)S(1)}, f32[32,192]{1,0:T(8,128)}, u32[]{:S(2)}) copy-start(f32[32,192]{1,0:T(8,128)} %get-tuple-element.102) | copy-start | bytes 73732
  99.3 8.1 %collective-permute-start.16 = (f32[1,8,32]{2,1,0:T(8,128)}, f32[1,8,32]{2,1,0:T(8,128)S(1)}, u32[]{:S(2)}, u32[]{:S(2)}) collective-permute-start(f32[1,8,32]{2,1,0:T(8,128)} %collective-permute-done.15), channel_id=1, source_target_pairs={{0,4},{4,8},{8,12},{12,16},{16,20},{20,24},{24,28},{28,0},{1,5},{5... | collective-permute-start | bytes 3080 | tf_op jit(solution)/shard_map/ppermute | solution.py:205
  107.5 6.4 %collective-permute-start.17 = (f32[1,8,32]{2,1,0:T(8,128)S(1)}, f32[1,8,32]{2,1,0:T(8,128)}, u32[]{:S(2)}, u32[]{:S(2)}) collective-permute-start(f32[1,8,32]{2,1,0:T(8,128)S(1)} %collective-permute-done.16), channel_id=1, source_target_pairs={{0,4},{4,8},{8,12},{12,16},{16,20},{20,24},{24,28},{28,0},{1,5},{5... | collective-permute-start | bytes 3080 | tf_op jit(solution)/shard_map/ppermute | solution.py:205
  113.9 6.5 %collective-permute-start.18 = (f32[1,8,32]{2,1,0:T(8,128)}, f32[1,8,32]{2,1,0:T(8,128)S(1)}, u32[]{:S(2)}, u32[]{:S(2)}) collective-permute-start(f32[1,8,32]{2,1,0:T(8,128)} %collective-permute-done.17), channel_id=1, source_target_pairs={{0,4},{4,8},{8,12},{12,16},{16,20},{20,24},{24,28},{28,0},{1,5},{5... | collective-permute-start | bytes 3080 | tf_op jit(solution)/shard_map/ppermute | solution.py:205
  129.6 4.7 %collective-permute-start = (f32[35,1024]{1,0:T(8,128)S(1)}, f32[35,1024]{1,0:T(8,128)S(1)}, u32[]{:S(2)}, u32[]{:S(2)}) collective-permute-start(f32[35,1024]{1,0:T(8,128)S(1)} %get-tuple-element.96), channel_id=1, source_target_pairs={{0,4},{4,8},{8,12},{12,16},{16,20},{20,24},{24,28},{1,5},{5,9},{9,... | collective-permute-start | bytes 430088 | tf_op jit(solution)/shard_map/ppermute | solution.py:22
  131.5 7.2 %collective-permute-start.1 = (f32[35,1024]{1,0:T(8,128)S(1)}, f32[35,1024]{1,0:T(8,128)S(1)}, u32[]{:S(2)}, u32[]{:S(2)}) collective-permute-start(f32[35,1024]{1,0:T(8,128)S(1)} %get-tuple-element.97), channel_id=1, source_target_pairs={{4,0},{8,4},{12,8},{16,12},{20,16},{24,20},{28,24},{5,1},{9,5},{13... | collective-permute-start | bytes 430088 | tf_op jit(solution)/shard_map/ppermute | solution.py:25
  246.8 22.0 %copy-start.3 = (f32[8,8192]{1,0:T(8,128)S(1)}, f32[8,8192]{1,0:T(8,128)}, u32[]{:S(2)}) copy-start(f32[8,8192]{1,0:T(8,128)} %param.40) | copy-start | bytes 786436
  247.8 22.0 %copy-start.1 = (f32[32,8192]{1,0:T(8,128)S(1)}, f32[32,8192]{1,0:T(8,128)}, u32[]{:S(2)}) copy-start(f32[32,8192]{1,0:T(8,128)} %all-gather.2.cloned.1.call-done) | copy-start | bytes 3145732
  269.8 22.9 %copy-start.5 = (f32[8,8192]{1,0:T(8,128)}, f32[8,8192]{1,0:T(8,128)S(1)}, u32[]{:S(2)}) copy-start(f32[8,8192]{1,0:T(8,128)S(1)} %multiply_add_fusion) | copy-start | bytes 786436
  (22 other events, 51.8 us)
Sparse Core Ops, SparseCore 0:
  18.3 19.1 all-gather.1
  243.7 25.0 reduce-scatter.1
